TPU v7x, 32 devices: a whole 2x2x4 slice. The times are simulated.
32 devices in a mesh: aux: 4 (over z), pair: 8 (over y, x, core).
Axes of the slice: x: 2, y: 2, z: 4, core: 2. Of those that a mesh axis runs over, the one named last changes fastest.
Arguments:
- metric: bfloat16 [4096, 4096], P('aux', 'pair'), may hold values from -0.09375 to 0.09375
- amplitudes: bfloat16 [4096, 16384], P('aux', 'pair'), may hold values from -0.59765625 to 0.59765625
- virt_coef: bfloat16 [1024, 1280], replicated, may hold values from -1.5 to 1.5
Outputs:
- density: float32 [4096, 4096], P('aux', 'pair')
- fitted_ao: bfloat16 [4096, 20480], P(('aux', 'pair'))
All inputs are finite; a program needn't handle non-finite values.
Results may differ from a plain program's by a relative error of at most 0.012.
Values may be sent and summed in bfloat16 or wider, within the bound.
A program may use at most 128 MiB of HBM per device.

v0:
```python
import jax
import jax.numpy as jnp
from jax import lax
from jax.sharding import PartitionSpec as P


def shards(metric, amplitudes, virt_coef):
    rows_metric = lax.all_gather(metric, "pair", axis=1, tiled=True)
    full_amp = lax.all_gather(amplitudes, "aux", axis=0, tiled=True)
    fitted = jnp.dot(rows_metric, full_amp, preferred_element_type=jnp.float32).astype(jnp.bfloat16)
    partial_value = lax.dot_general(
        fitted, full_amp, (((1,), (1,)), ((), ())), preferred_element_type=jnp.float32
    )
    density = lax.psum_scatter(
        partial_value.astype(jnp.bfloat16), "pair", scatter_dimension=1, tiled=True
    ).astype(jnp.float32)
    regrouped = lax.all_to_all(fitted, "pair", split_axis=0, concat_axis=1, tiled=True)
    row_count = regrouped.shape[0]
    virt_count = virt_coef.shape[0]
    ao_count = virt_coef.shape[1]
    occ_count = regrouped.shape[1] // virt_count
    blocks = regrouped.reshape(row_count * occ_count, virt_count)
    fitted_ao = jnp.dot(blocks, virt_coef, preferred_element_type=jnp.float32).astype(jnp.bfloat16)
    return (density, fitted_ao.reshape(row_count, occ_count * ao_count))


def solution(mesh):
    in_specs = (P("aux", "pair"), P("aux", "pair"), P())
    out_specs = (P("aux", "pair"), P(("aux", "pair"), None))
    return jax.shard_map(shards, mesh=mesh, in_specs=in_specs, out_specs=out_specs, check_vma=False)
```

profile of v0, /device:TPU:0, one launch (start us, length us, event | category | flops | bytes accessed | tf_op | source)
XLA Modules:
  0.0 516.1 jit_solution(2569435131899505442)
XLA Ops:
  7.2 0.0 copy-start
  7.2 0.0 all-gather.3.cloned.1.call-start
  7.2 0.7 all-gather.3.cloned.1.call-update
  7.9 0.0 all-gather.5.cloned.1.call-start
  8.0 0.7 all-gather.5.cloned.1.call-update
  8.7 0.0 reduce-scatter.2.cloned.1.call-start
  8.7 59.8 %all-gather.3.cloned.1.call-done = bf16[1024,4096]{1,0:T(8,128)(2,1)} async-done(((bf16[1024,512]{1,0:T(8,128)(2,1)}), bf16[1024,4096]{1,0:T(8,128)(2,1)}) %all-gather.3.cloned.1.call-update) | async-done | bytes 8388624 | tf_op jit(solution)/shard_map/all_gather | solution.py:8
  68.5 288.4 %all-gather.5.cloned.1.call-done = bf16[4096,2048]{1,0:T(8,128)(2,1)} async-done(((bf16[1024,2048]{1,0:T(8,128)(2,1)}), bf16[4096,2048]{1,0:T(8,128)(2,1)}) %all-gather.5.cloned.1.call-update) | async-done | bytes 16777232 | tf_op jit(solution)/shard_map/all_gather | solution.py:9
  356.8 0.0 copy-start.2
  356.8 22.8 %fusion.1 = bf16[1024,2048]{1,0:T(8,128)(2,1)S(1)} fusion(bf16[1024,4096]{1,0:T(8,128)(2,1)} %all-gather.3.cloned.1.call-done, bf16[4096,2048]{1,0:T(8,128)(2,1)} %all-gather.5.cloned.1.call-done), kind=kOutput, calls=%fused_computation.3 | convolution fusion | flops 17179869184 | bytes 29360128 | tf_op jit(solution)/shard_map/dot_general | solution.py:10
  379.7 0.0 copy-start.1
  379.7 2.0 copy-done.1
  381.7 0.0 copy-done.2
  381.7 19.6 %convolution_convert_fusion.1 = bf16[1024,4096]{1,0:T(8,128)(2,1)} fusion(bf16[4096,2048]{1,0:T(8,128)(2,1)S(1)} %copy-done.2, bf16[1024,2048]{1,0:T(8,128)(2,1)S(1)} %fusion.1), kind=kOutput, calls=%fused_computation.1 | convolution fusion | flops 17184063488 | bytes 29360128 | tf_op jit(solution)/shard_map/dot_general | solution.py:11
  401.2 0.0 reduce-scatter.2.cloned.1.call-update
  401.3 75.2 %all_to_all.16 = bf16[8,128,2048]{2,1,0:T(8,128)(2,1)S(1)} all-to-all(bf16[8,128,2048]{2,1,0:T(8,128)(2,1)} %bitcast.9), channel_id=1, replica_groups=mesh['aux'=4,'pair'=8] {'pair'}, dimensions={0} | all-to-all | bytes 8388608 | tf_op jit(solution)/shard_map/all_to_all | solution.py:17
  476.4 4.4 copy.6
  480.8 7.1 %reshape.14 = bf16[2048,1024]{1,0:T(8,128)(2,1)} reshape(bf16[128,8,2048]{2,1,0:T(8,128)(2,1)} %copy.6) | data formatting | bytes 8388608 | tf_op jit(solution)/shard_map/reshape | solution.py:22
  487.9 0.0 copy-done
  487.9 10.8 %convolution_convert_fusion = bf16[2048,1280]{1,0:T(8,128)(2,1)} fusion(bf16[2048,1024]{1,0:T(8,128)(2,1)} %reshape.14, bf16[1024,1280]{1,0:T(8,128)(2,1)S(1)} %copy-done), kind=kOutput, calls=%fused_computation | convolution fusion | flops 5371330560 | bytes 12058624 | tf_op jit(solution)/shard_map/dot_general | solution.py:23
  498.7 8.1 %reshape.15 = bf16[128,20480]{1,0:T(8,128)(2,1)} reshape(bf16[2048,1280]{1,0:T(8,128)(2,1)} %convolution_convert_fusion) | data formatting | bytes 10485760 | tf_op jit(solution)/shard_map/reshape | solution.py:24
  506.7 0.0 reduce-scatter.2.cloned.1.call-done
  506.7 2.8 convert_element_type.14
Async XLA Ops:
  7.2 480.7 %copy-start = (bf16[1024,1280]{1,0:T(8,128)(2,1)S(1)}, bf16[1024,1280]{1,0:T(8,128)(2,1)}, u32[]{:S(2)}) copy-start(bf16[1024,1280]{1,0:T(8,128)(2,1)} %param.5) | copy-start | bytes 7864324
  7.2 61.3 %all-gather.3.cloned.1.call-start = ((), (), s32[]{:S(2)}) async-start(), calls=%async_computation.2 | async-start | bytes 9437184 | tf_op jit(solution)/shard_map/all_gather | solution.py:8
  7.9 348.9 %all-gather.5.cloned.1.call-start = ((), (), s32[]{:S(2)}) async-start(), calls=%async_computation.3 | async-start | bytes 20971520 | tf_op jit(solution)/shard_map/all_gather | solution.py:9
  8.7 498.0 %reduce-scatter.2.cloned.1.call-start = ((), (), s32[]{:S(2)}) async-start(), calls=%async_computation.4 | async-start | bytes 9437184 | tf_op jit(solution)/shard_map/reduce_scatter | solution.py:14
  356.8 24.9 %copy-start.2 = (bf16[4096,2048]{1,0:T(8,128)(2,1)S(1)}, bf16[4096,2048]{1,0:T(8,128)(2,1)}, u32[]{:S(2)}) copy-start(bf16[4096,2048]{1,0:T(8,128)(2,1)} %all-gather.5.cloned.1.call-done) | copy-start | bytes 50331652
  379.7 2.0 copy-start.1
Sparse Core Ops, SparseCore 0:
  9.9 58.5 all-gather.2
  70.0 286.7 all-gather.4
  401.4 92.9 reduce-scatter.1
where the time goes:
time: 517 us; the launch traced here: 516 us
  waiting for transfers between devices  350 us (68%)
  blocking collectives  75.2 us (15%)
  matrix products  53.1 us (10%)
  local copies, waits for them, and re-layouts  21.5 us (4%)
  between operations  13.8 us (3%)
    all_gather x1, waiting for transfers between devices, shards(): full_amp = lax.all_gather(amplitudes, 'aux', axis=0, tiled=True)  288 us
    all_to_all x1, blocking collectives, shards(): lax.all_to_all(fitted, 'pair', split_axis=0, concat_axis=1, tiled=True)  75.2 us
    all_gather x1, waiting for transfers between devices, shards(): rows_metric = lax.all_gather(metric, 'pair', axis=1, tiled=True)  59.8 us
    dot_general x1, matrix products, shards(): jnp.dot(rows_metric, full_amp, preferred_element_type=jnp.float32)  22.8 us
    dot_general x1, matrix products, shards(): lax.dot_general(fitted, full_amp, (((1,), (1,)), ((), ())), preferred_ele...  19.6 us
    dot_general x1, matrix products, shards(): jnp.dot(blocks, virt_coef, preferred_element_type=jnp.float32)  10.8 us
  transfers between devices with their start and end apart: 3, of which 2 were waited for; matrix products, arithmetic and copies ran while one was open for 6% of the time, Pallas kernels for 0%

commit v1 on v0

v1 whole, which is shorter than its diff:
```python
import functools

import jax
import jax.numpy as jnp
from jax import lax
from jax.experimental import pallas as pl
from jax.experimental.pallas import tpu as pltpu
from jax.sharding import PartitionSpec as P

MESH = pl.DeviceIdType.MESH


def kernel(
    na, n, count, metric, amp, virt_coef, density, fitted_ao,
    m_v, a_v, d_v, f_v, g_v, c_v, one_v, two_v, o_v,
    m_send, m_recv, z_send, z_recv, x_send, x_recv, one_send, one_recv, two_send, two_recv, o_sem, local_sem,
):
    a, b = lax.axis_index("aux"), lax.axis_index("pair")
    p, q = metric.shape
    per = amp.shape[1]
    w = per // count
    rows = p // n
    virt, ao = virt_coef.shape
    half = n // 2
    parity, chip = lax.rem(b, 2), b // 2
    partner = b + 1 - 2 * parity
    tile = min(256, p)
    tiles = p // tile

    barrier = pltpu.get_barrier_semaphore()
    for d in range(1, n):
        pl.semaphore_signal(barrier, inc=1, device_id=(a, lax.rem(b + d, n)), device_id_type=MESH)

    @pl.when(a > 0)
    def _():
        pl.semaphore_signal(barrier, inc=1, device_id=(a - 1, b), device_id_type=MESH)

    @pl.when(a < na - 1)
    def _():
        pl.semaphore_signal(barrier, inc=1, device_id=(a + 1, b), device_id_type=MESH)

    pl.semaphore_wait(barrier, n - 1 + jnp.where(a > 0, 1, 0) + jnp.where(a < na - 1, 1, 0))

    def block_of(s, c):
        return a_v.at[c, pl.ds(pl.multiple_of(s * p, p), p), :]

    def hop(src, s, c, way, target):
        return pltpu.make_async_remote_copy(
            src_ref=src, dst_ref=block_of(s, c), send_sem=z_send.at[way, s, c],
            recv_sem=z_recv.at[s, c], device_id=(target, b), device_id_type=MESH,
        )

    def metric_copy(owner, target):
        return pltpu.make_async_remote_copy(
            src_ref=metric, dst_ref=m_v.at[:, pl.ds(pl.multiple_of(owner * q, q), q)],
            send_sem=m_send.at[target], recv_sem=m_recv.at[owner],
            device_id=(a, target), device_id_type=MESH,
        )

    def regroup(owner, target, c):
        return pltpu.make_async_remote_copy(
            src_ref=f_v.at[c, pl.ds(pl.multiple_of(target * rows, rows), rows), :],
            dst_ref=g_v.at[:, pl.ds(pl.multiple_of(owner * per + c * w, w), w)],
            send_sem=x_send.at[target, c], recv_sem=x_recv.at[owner, c],
            device_id=(a, target), device_id_type=MESH,
        )

    def staged(j):
        return m_v.at[:, pl.ds(pl.multiple_of(j * q, q), q)]

    def first(j):
        return pltpu.make_async_remote_copy(
            src_ref=staged(j), dst_ref=one_v.at[j // 2], send_sem=one_send.at[j // 2],
            recv_sem=one_recv.at[j // 2], device_id=(a, partner), device_id_type=MESH,
        )

    def second(source, j):
        return pltpu.make_async_remote_copy(
            src_ref=staged(j), dst_ref=two_v.at[source], send_sem=two_send.at[j // 2],
            recv_sem=two_recv.at[source], device_id=(a, j), device_id_type=MESH,
        )

    def mine(c):
        return amp.at[:, c * w : (c + 1) * w]

    for c in range(count):
        @pl.when(a > 0)
        def _():
            hop(mine(c), a, c, 0, jnp.maximum(a - 1, 0)).start()

        @pl.when(a < na - 1)
        def _():
            hop(mine(c), a, c, 1, jnp.minimum(a + 1, na - 1)).start()

    @pl.loop(1, n)
    def _(d):
        metric_copy(b, lax.rem(b + d, n)).start()

    own_copies = [pltpu.make_async_copy(mine(c), block_of(a, c), local_sem.at[c]) for c in range(count)]
    own_copies.append(pltpu.make_async_copy(metric, staged(b), local_sem.at[count]))
    own_copies.append(pltpu.make_async_copy(virt_coef, c_v, local_sem.at[count + 1]))
    for copy in own_copies:
        copy.start()

    def arrive(t, c):
        @pl.when(a - t >= 0)
        def _():
            s = jnp.maximum(a - t, 0)
            hop(block_of(s, c), s, c, 1, a).wait_recv()

            @pl.when(a < na - 1)
            def _():
                hop(block_of(s, c), s, c, 1, jnp.minimum(a + 1, na - 1)).start()

        @pl.when(a + t < na)
        def _():
            s = jnp.minimum(a + t, na - 1)
            hop(block_of(s, c), s, c, 0, a).wait_recv()

            @pl.when(a > 0)
            def _():
                hop(block_of(s, c), s, c, 0, jnp.maximum(a - 1, 0)).start()

    @pl.loop(1, na - 1)
    def _(t):
        @pl.loop(0, count)
        def _(c):
            arrive(t, c)

    for copy in own_copies:
        copy.wait()

    @pl.loop(1, n)
    def _(d):
        metric_copy(lax.rem(b + n - d, n), b).wait_recv()

    @pl.loop(1, n)
    def _(d):
        metric_copy(b, lax.rem(b + d, n)).wait_send()

    def row(r):
        return pl.ds(pl.multiple_of(r * tile, tile), tile)

    def product(j, r, c):
        right = a_v[c, pl.ds(pl.multiple_of(j * q, q), q), :]
        return lax.dot_general(
            f_v[c, row(r), :], right, (((1,), (1,)), ((), ())), preferred_element_type=jnp.float32
        )

    def fit(c):
        @pl.loop(0, tiles)
        def _(r):
            f_v[c, row(r), :] = jnp.dot(
                m_v[row(r), :], a_v[c], preferred_element_type=jnp.float32
            ).astype(f_v.dtype)

        @pl.loop(1, n)
        def _(d):
            regroup(b, lax.rem(b + d, n), c).start()

        pltpu.make_async_copy(
            f_v.at[c, pl.ds(pl.multiple_of(b * rows, rows), rows), :],
            g_v.at[:, pl.ds(pl.multiple_of(b * per + c * w, w), w)], x_send.at[b, c],
        ).start()

    @pl.loop(0, n * tiles)
    def _(i):
        d_v[i // tiles, row(lax.rem(i, tiles)), :] = jnp.zeros((tile, q), jnp.float32)

    @pl.loop(0, count - 1)
    def _(c):
        arrive(na - 1, c)
        fit(c)

        @pl.loop(0, n * tiles)
        def _(i):
            j, r = i // tiles, lax.rem(i, tiles)
            d_v[j, row(r), :] += product(j, r, c)

    last = count - 1
    arrive(na - 1, last)
    fit(last)

    @pl.loop(0, half)
    def _(h):
        j = 2 * lax.rem(chip + h, half) + 1 - parity

        @pl.loop(0, tiles)
        def _(r):
            m_v[row(r), pl.ds(pl.multiple_of(j * q, q), q)] = (
                d_v[j, row(r), :] + product(j, r, last)
            ).astype(m_v.dtype)

        first(j).start()

    @pl.loop(0, half)
    def _(h):
        j = 2 * lax.rem(chip + h, half) + parity

        @pl.loop(0, tiles)
        def _(r):
            d_v[j, row(r), :] += product(j, r, last)

    @pl.loop(1, half)
    def _(h):
        slot = lax.rem(chip + h, half)
        j = 2 * slot + parity
        first(j).wait_recv()

        @pl.loop(0, tiles)
        def _(r):
            m_v[row(r), pl.ds(pl.multiple_of(j * q, q), q)] = (
                d_v[j, row(r), :] + one_v[slot, row(r), :].astype(jnp.float32)
            ).astype(m_v.dtype)

        second(chip, j).start()

    first(b).wait_recv()

    @pl.loop(0, tiles)
    def _(r):
        d_v[b, row(r), :] += one_v[chip, row(r), :].astype(jnp.float32)

    @pl.loop(0, count)
    def _(c):
        pltpu.make_async_copy(
            f_v.at[c, pl.ds(pl.multiple_of(b * rows, rows), rows), :],
            g_v.at[:, pl.ds(pl.multiple_of(b * per + c * w, w), w)], x_send.at[b, c],
        ).wait()

        @pl.loop(1, n)
        def _(d):
            regroup(lax.rem(b + n - d, n), b, c).wait_recv()

    occ = n * per // virt

    def out_copy(i, slot):
        return pltpu.make_async_copy(
            o_v.at[slot], fitted_ao.at[:, pl.ds(pl.multiple_of(i * ao, ao), ao)], o_sem.at[slot]
        )

    @pl.loop(0, occ)
    def _(i):
        slot = lax.rem(i, 2)

        @pl.when(i >= 2)
        def _():
            out_copy(i - 2, slot).wait()

        o_v[slot] = jnp.dot(
            g_v[:, pl.ds(pl.multiple_of(i * virt, virt), virt)], c_v[...], preferred_element_type=jnp.float32
        ).astype(o_v.dtype)
        out_copy(i, slot).start()

    for i in range(max(occ - 2, 0), occ):
        out_copy(i, i % 2).wait()

    @pl.loop(1, half)
    def _(h):
        source = lax.rem(chip + half - h, half)
        second(source, b).wait_recv()

        @pl.loop(0, tiles)
        def _(r):
            d_v[b, row(r), :] += two_v[source, row(r), :].astype(jnp.float32)

    result = pltpu.make_async_copy(d_v.at[b], density, local_sem.at[0])
    result.start()

    @pl.loop(0, half)
    def _(h):
        first(2 * h + 1 - parity).wait_send()

    @pl.loop(1, half)
    def _(h):
        second(chip, 2 * lax.rem(chip + h, half) + parity).wait_send()

    @pl.loop(0, count)
    def _(c):
        @pl.loop(1, n)
        def _(d):
            regroup(b, lax.rem(b + d, n), c).wait_send()

        @pl.loop(0, na)
        def _(s):
            @pl.when(jnp.logical_and(s >= a, a > 0))
            def _():
                hop(block_of(s, c), s, c, 0, jnp.maximum(a - 1, 0)).wait_send()

            @pl.when(jnp.logical_and(s <= a, a < na - 1))
            def _():
                hop(block_of(s, c), s, c, 1, jnp.minimum(a + 1, na - 1)).wait_send()

    result.wait()


def shards(na, n, metric, amplitudes, virt_coef):
    p, q = metric.shape
    per = amplitudes.shape[1]
    virt, ao = virt_coef.shape
    count = 4
    w = per // count
    rows = p // n
    bf16 = jnp.bfloat16
    dma = pltpu.SemaphoreType.DMA
    return pl.pallas_call(
        functools.partial(kernel, na, n, count),
        out_shape=(
            jax.ShapeDtypeStruct((p, q), jnp.float32),
            jax.ShapeDtypeStruct((rows, n * per // virt * ao), bf16),
        ),
        in_specs=[pl.BlockSpec(memory_space=pl.ANY)] * 3,
        out_specs=(pl.BlockSpec(memory_space=pl.ANY), pl.BlockSpec(memory_space=pl.ANY)),
        scratch_shapes=[
            pltpu.VMEM((p, n * q), bf16),
            pltpu.VMEM((count, na * p, w), bf16),
            pltpu.VMEM((n, p, q), jnp.float32),
            pltpu.VMEM((count, p, w), bf16),
            pltpu.VMEM((rows, n * per), bf16),
            pltpu.VMEM((virt, ao), bf16),
            pltpu.VMEM((n // 2, p, q), bf16),
            pltpu.VMEM((n // 2, p, q), bf16),
            pltpu.VMEM((2, rows, ao), bf16),
            dma((n,)), dma((n,)),
            dma((2, na, count)), dma((na, count)),
            dma((n, count)), dma((n, count)),
            dma((n // 2,)), dma((n // 2,)),
            dma((n // 2,)), dma((n // 2,)),
            dma((2,)), dma((count + 2,)),
        ],
        compiler_params=pltpu.CompilerParams(
            collective_id=0, has_side_effects=True, vmem_limit_bytes=67043328
        ),
    )(metric, amplitudes, virt_coef)


def solution(mesh):
    in_specs = (P("aux", "pair"), P("aux", "pair"), P())
    out_specs = (P("aux", "pair"), P(("aux", "pair"), None))
    body = functools.partial(shards, mesh.shape["aux"], mesh.shape["pair"])
    return jax.shard_map(body, mesh=mesh, in_specs=in_specs, out_specs=out_specs, check_vma=False)
```

time: 517 us -> 351 us (0.68)
  waiting for transfers between devices: 350 us -> 0 us
  Pallas kernels: 0 us -> 342 us
  blocking collectives: 75.2 us -> 0 us
  matrix products: 53.1 us -> 0 us
  between operations: 13.8 us -> 0.64 us
  local copies, waits for them, and re-layouts: 21.5 us -> 8.39 us
    all_gather x2 -> x0, waiting for transfers between devices: 348 us -> none  [the longest x1 288 us: shards(): full_amp = lax.all_gather(amplitudes, 'aux', axis=0, tiled=True)]
    pallas_call x0 -> x1, Pallas kernels: none -> 342 us  [shards(): pl.pallas_call(functools.partial(kernel, na, n, count), out_shape=(jax.Sh...]
    all_to_all x1 -> x0, blocking collectives: 75.2 us -> none  [shards(): lax.all_to_all(fitted, 'pair', split_axis=0, concat_axis=1, tiled=True)]
    dot_general x3 -> x0, matrix products: 53.1 us -> none  [the longest x1 22.8 us: shards(): jnp.dot(rows_metric, full_amp, preferred_element_type=jnp.float32)]
    reshape x2 -> x0, local copies, waits for them, and re-layouts: 15.2 us -> none  [the longest x1 8.06 us: shards(): return (density, fitted_ao.reshape(row_count, occ_count * ao_count))]
    unnamed x6 -> x2, local copies, waits for them, and re-layouts: 2.02 us -> 8.39 us
  transfers between devices with their start and end apart: 3 -> 0, of which waited for: 2 -> 0; matrix products, arithmetic and copies ran while one was open for 6% -> 0% of each run, Pallas kernels for 0% -> 0%
where the time goes in v1:
time: 351 us
  Pallas kernels  342 us (97%)
  local copies, waits for them, and re-layouts  8.39 us (2%)
    pallas_call x1, Pallas kernels, shards(): pl.pallas_call(functools.partial(kernel, na, n, count), out_shape=(jax.Sh...  342 us
    unnamed x2, local copies, waits for them, and re-layouts  8.39 us

profile of v1, /device:TPU:0, one launch (start us, length us, event | category | flops | bytes accessed | tf_op | source)
XLA Modules:
  0.0 350.5 jit_solution(15086850280681889687)
XLA Ops:
  0.6 341.5 %shard_map.50 = (f32[1024,512]{1,0:T(8,128)}, bf16[128,20480]{1,0:T(8,128)(2,1)}) custom-call(bf16[1024,512]{1,0:T(8,128)(2,1)} %metric.1, bf16[1024,2048]{1,0:T(8,128)(2,1)} %amp.1, bf16[1024,1280]{1,0:T(8,128)(2,1)} %virt_coef.1), custom_call_target="tpu_custom_call" | custom-call | tf_op jit(solution)/shard_map/pallas_call | solution.py:306
  342.2 3.1 copy.7
  345.2 5.3 %copy.8 = bf16[128,20480]{1,0:T(8,128)(2,1)} copy(bf16[128,20480]{1,0:T(8,128)(2,1)} %get-tuple-element.5) | data formatting | bytes 10485760

commit v2 on v1

--- a/solution.py
+++ b/solution.py
@@ -76,8 +76,8 @@
 
     def second(source, j):
         return pltpu.make_async_remote_copy(
-            src_ref=staged(j), dst_ref=two_v.at[source], send_sem=two_send.at[j // 2],
-            recv_sem=two_recv.at[source], device_id=(a, j), device_id_type=MESH,
+            src_ref=staged(j), dst_ref=two_v.at[source], send_sem=two_send.at[0, j // 2],
+            recv_sem=two_recv.at[0, source], device_id=(a, j), device_id_type=MESH,
         )
 
     def mine(c):
@@ -201,25 +201,75 @@
         def _(r):
             d_v[j, row(r), :] += product(j, r, last)
 
-    @pl.loop(1, half)
-    def _(h):
-        slot = lax.rem(chip + h, half)
+    quad = half == 4
+    mid = p // 2
+    near = (chip + 1 - 2 * lax.rem(chip, 2), lax.rem(chip + 2, 4))
+    far = 3 - chip
+
+    def part(way):
+        return pl.ds(way * mid, mid)
+
+    def cast(slot, way):
         j = 2 * slot + parity
-        first(j).wait_recv()
+        m_v[part(way), pl.ds(pl.multiple_of(j * q, q), q)] = d_v[j, part(way), :].astype(m_v.dtype)
+
+    def piece(slot, way, place, target):
+        j = 2 * slot + parity
+        return pltpu.make_async_remote_copy(
+            src_ref=m_v.at[part(way), pl.ds(pl.multiple_of(j * q, q), q)],
+            dst_ref=two_v.at[place, part(way), :], send_sem=two_send.at[way, place],
+            recv_sem=two_recv.at[way, place], device_id=(a, 2 * target + parity), device_id_type=MESH,
+        )
+
+    def add_in(slot, place, way):
+        j = 2 * slot + parity
+        d_v[j, part(way), :] += two_v[place, part(way), :].astype(jnp.float32)
+
+    if quad:
+        for h in range(4):
+            slot = (far, near[0], near[1], chip)[h]
+            first(2 * slot + parity).wait_recv()
+
+            @pl.loop(0, tiles)
+            def _(r, slot=slot):
+                j = 2 * slot + parity
+                d_v[j, row(r), :] += one_v[slot, row(r), :].astype(jnp.float32)
+
+            if h == 0:
+                for way in range(2):
+                    cast(far, way)
+                    piece(far, way, 0, near[way]).start()
+            elif h < 3:
+                cast(near[h - 1], h - 1)
+                piece(near[h - 1], h - 1, 1, near[h - 1]).start()
+    else:
+        @pl.loop(1, half)
+        def _(h):
+            slot = lax.rem(chip + h, half)
+            j = 2 * slot + parity
+            first(j).wait_recv()
+
+            @pl.loop(0, tiles)
+            def _(r):
+                m_v[row(r), pl.ds(pl.multiple_of(j * q, q), q)] = (
+                    d_v[j, row(r), :] + one_v[slot, row(r), :].astype(jnp.float32)
+                ).astype(m_v.dtype)
+
+            second(chip, j).start()
+
+        first(b).wait_recv()
 
         @pl.loop(0, tiles)
         def _(r):
-            m_v[row(r), pl.ds(pl.multiple_of(j * q, q), q)] = (
-                d_v[j, row(r), :] + one_v[slot, row(r), :].astype(jnp.float32)
-            ).astype(m_v.dtype)
-
-        second(chip, j).start()
-
-    first(b).wait_recv()
-
-    @pl.loop(0, tiles)
-    def _(r):
-        d_v[b, row(r), :] += one_v[chip, row(r), :].astype(jnp.float32)
+            d_v[b, row(r), :] += one_v[chip, row(r), :].astype(jnp.float32)
+
+    if quad:
+        for way in range(2):
+            other = near[1 - way]
+            piece(other, way, 0, near[way]).wait_recv()
+            add_in(other, 0, way)
+            cast(other, way)
+            piece(other, way, 2, other).start()
 
     @pl.loop(0, count)
     def _(c):
@@ -255,14 +305,22 @@
     for i in range(max(occ - 2, 0), occ):
         out_copy(i, i % 2).wait()
 
-    @pl.loop(1, half)
-    def _(h):
-        source = lax.rem(chip + half - h, half)
-        second(source, b).wait_recv()
-
-        @pl.loop(0, tiles)
-        def _(r):
-            d_v[b, row(r), :] += two_v[source, row(r), :].astype(jnp.float32)
+    if quad:
+        for way in range(2):
+            piece(chip, way, 1, near[way]).wait_recv()
+            add_in(chip, 1, way)
+        for way in range(2):
+            piece(chip, way, 2, near[1 - way]).wait_recv()
+            add_in(chip, 2, way)
+    else:
+        @pl.loop(1, half)
+        def _(h):
+            source = lax.rem(chip + half - h, half)
+            second(source, b).wait_recv()
+
+            @pl.loop(0, tiles)
+            def _(r):
+                d_v[b, row(r), :] += two_v[source, row(r), :].astype(jnp.float32)
 
     result = pltpu.make_async_copy(d_v.at[b], density, local_sem.at[0])
     result.start()
@@ -271,9 +329,15 @@
     def _(h):
         first(2 * h + 1 - parity).wait_send()
 
-    @pl.loop(1, half)
-    def _(h):
-        second(chip, 2 * lax.rem(chip + h, half) + parity).wait_send()
+    if quad:
+        for way in range(2):
+            piece(far, way, 0, near[way]).wait_send()
+            piece(near[way], way, 1, near[way]).wait_send()
+            piece(near[1 - way], way, 2, near[1 - way]).wait_send()
+    else:
+        @pl.loop(1, half)
+        def _(h):
+            second(chip, 2 * lax.rem(chip + h, half) + parity).wait_send()
 
     @pl.loop(0, count)
     def _(c):
@@ -298,7 +362,7 @@
     p, q = metric.shape
     per = amplitudes.shape[1]
     virt, ao = virt_coef.shape
-    count = 4
+    count = next(c for c in (8, 4, 2, 1) if per % (128 * c) == 0)
     w = per // count
     rows = p // n
     bf16 = jnp.bfloat16
@@ -325,7 +389,7 @@
             dma((2, na, count)), dma((na, count)),
             dma((n, count)), dma((n, count)),
             dma((n // 2,)), dma((n // 2,)),
-            dma((n // 2,)), dma((n // 2,)),
+            dma((2, n // 2)), dma((2, n // 2)),
             dma((2,)), dma((count + 2,)),
         ],
         compiler_params=pltpu.CompilerParams(

time: 351 us -> 339 us (0.966)
  Pallas kernels: 342 us -> 330 us
    pallas_call x1, Pallas kernels: 342 us -> 330 us  [shards(): pl.pallas_call(functools.partial(kernel, na, n, count), out_shape=(jax.Sh...]
where the time goes in v2:
time: 339 us
  Pallas kernels  330 us (97%)
  local copies, waits for them, and re-layouts  8.39 us (2%)
    pallas_call x1, Pallas kernels, shards(): pl.pallas_call(functools.partial(kernel, na, n, count), out_shape=(jax.Sh...  330 us
    unnamed x2, local copies, waits for them, and re-layouts  8.39 us

profile of v2, /device:TPU:0, one launch (start us, length us, event | category | flops | bytes accessed | tf_op | source)
XLA Modules:
  0.0 339.2 jit_solution(11728704364434000654)
XLA Ops:
  0.6 330.2 %shard_map.50 = (f32[1024,512]{1,0:T(8,128)}, bf16[128,20480]{1,0:T(8,128)(2,1)}) custom-call(bf16[1024,512]{1,0:T(8,128)(2,1)} %metric.1, bf16[1024,2048]{1,0:T(8,128)(2,1)} %amp.1, bf16[1024,1280]{1,0:T(8,128)(2,1)} %virt_coef.1), custom_call_target="tpu_custom_call" | custom-call | tf_op jit(solution)/shard_map/pallas_call | solution.py:370
  330.8 3.1 copy.7
  333.9 5.3 %copy.8 = bf16[128,20480]{1,0:T(8,128)(2,1)} copy(bf16[128,20480]{1,0:T(8,128)(2,1)} %get-tuple-element.5) | data formatting | bytes 10485760

commit v3 on v2

--- a/solution.py
+++ b/solution.py
@@ -181,9 +181,19 @@
     arrive(na - 1, last)
     fit(last)
 
+    quad = half == 4
+    mid = p // 2
+    near = (chip + 1 - 2 * lax.rem(chip, 2), lax.rem(chip + 2, 4))
+    far = 3 - chip
+
+    def turn(h):
+        if not quad:
+            return lax.rem(chip + h, half)
+        return jnp.where(h == 0, far, jnp.where(h == 1, near[0], jnp.where(h == 2, near[1], chip)))
+
     @pl.loop(0, half)
     def _(h):
-        j = 2 * lax.rem(chip + h, half) + 1 - parity
+        j = 2 * turn(h) + 1 - parity
 
         @pl.loop(0, tiles)
         def _(r):
@@ -193,7 +203,7 @@
 
         first(j).start()
 
-    @pl.loop(0, half)
+    @pl.loop(0, 0 if quad else half)
     def _(h):
         j = 2 * lax.rem(chip + h, half) + parity
 
@@ -201,11 +211,6 @@
         def _(r):
             d_v[j, row(r), :] += product(j, r, last)
 
-    quad = half == 4
-    mid = p // 2
-    near = (chip + 1 - 2 * lax.rem(chip, 2), lax.rem(chip + 2, 4))
-    far = 3 - chip
-
     def part(way):
         return pl.ds(way * mid, mid)
 
@@ -228,6 +233,11 @@
     if quad:
         for h in range(4):
             slot = (far, near[0], near[1], chip)[h]
+
+            @pl.loop(0, tiles)
+            def _(r, slot=slot):
+                d_v[2 * slot + parity, row(r), :] += product(2 * slot + parity, r, last)
+
             first(2 * slot + parity).wait_recv()
 
             @pl.loop(0, tiles)

time: 339 us -> 335 us (0.988)
  Pallas kernels: 330 us -> 326 us
    pallas_call x1, Pallas kernels: 330 us -> 326 us  [shards(): pl.pallas_call(functools.partial(kernel, na, n, count), out_shape=(jax.Sh...]
where the time goes in v3:
time: 335 us
  Pallas kernels  326 us (97%)
  local copies, waits for them, and re-layouts  8.39 us (3%)
    pallas_call x1, Pallas kernels, shards(): pl.pallas_call(functools.partial(kernel, na, n, count), out_shape=(jax.Sh...  326 us
    unnamed x2, local copies, waits for them, and re-layouts  8.39 us

profile of v3, /device:TPU:0, one launch (start us, length us, event | category | flops | bytes accessed | tf_op | source)
XLA Modules:
  0.0 335.1 jit_solution(17755321737464218796)
XLA Ops:
  0.6 326.1 %shard_map.50 = (f32[1024,512]{1,0:T(8,128)}, bf16[128,20480]{1,0:T(8,128)(2,1)}) custom-call(bf16[1024,512]{1,0:T(8,128)(2,1)} %metric.1, bf16[1024,2048]{1,0:T(8,128)(2,1)} %amp.1, bf16[1024,1280]{1,0:T(8,128)(2,1)} %virt_coef.1), custom_call_target="tpu_custom_call" | custom-call | tf_op jit(solution)/shard_map/pallas_call | solution.py:380
  326.7 3.1 copy.7
  329.8 5.3 %copy.8 = bf16[128,20480]{1,0:T(8,128)(2,1)} copy(bf16[128,20480]{1,0:T(8,128)(2,1)} %get-tuple-element.5) | data formatting | bytes 10485760
